TPU v7x, 32 devices: a whole 2x2x4 slice. The times are simulated.
32 devices in a mesh: pipe: 2 (over x), expert: 16 (over z, y, core).
Axes of the slice: x: 2, y: 2, z: 4, core: 2. Of those that a mesh axis runs over, the one named last changes fastest.
Arguments:
- inputs: bfloat16 [1, 512, 5120], P(None, 'expert'), may hold values from -6 to 6
- router: bfloat16 [2, 5120, 2], P('pipe'), may hold values from -0.078125 to 0.078125
- w_up: bfloat16 [2, 3072, 5120], P('pipe', 'expert'), may hold values from -0.078125 to 0.078125
- w_down: bfloat16 [2, 3072, 5120], P('pipe', 'expert'), may hold values from -0.15625 to 0.15625
- picks: int32 [2, 1, 2, 8], P('pipe'), may hold values from 0 to 511, as said below
- probe: bfloat16 [2, 64, 5120], P('pipe'), may hold values from -0.078125 to 0.078125
Outputs:
- student_feats: bfloat16 [2, 1, 512, 64], P('pipe', None, 'expert')
Inputs may be any that keep to these rules, and one draw needn't show every extreme that they name: Each list picks[s, m, e] holds 8 different token positions of the micro-batch. Of the 32 consecutive positions held by one index of expert, at most 1 stand in one list, and in every list some index has exactly 1.
All inputs are finite; a program needn't handle non-finite values.
Results may differ from a plain program's by a relative error of at most 0.0059.
Values may be sent and summed in bfloat16 or wider, within the bound.
A program may use at most 64 MiB of HBM per device.

v0:
```python
import jax
import jax.numpy as jnp
from jax import lax
from jax.sharding import PartitionSpec as P

SLOT = 1


def passed_along(x, axis, by):
    size = lax.axis_size(axis)
    pairs = [(i, i + by) for i in range(size) if 0 <= i + by < size]
    return lax.ppermute(x, axis, pairs)


def from_root(x, axis, root):
    mine = lax.axis_index(axis) == root
    return lax.psum(jnp.where(mine, x, jnp.zeros_like(x)), axis)


def rms_rows(rows_in):
    wide = rows_in.astype(jnp.float32)
    scale = lax.rsqrt(jnp.mean(wide * wide, axis=-1, keepdims=True) + 1e-06)
    return (wide * scale).astype(jnp.bfloat16)


def shards(inputs, router, w_up, w_down, picks, probe):
    sections = lax.axis_size("pipe")
    expert_width = lax.axis_size("expert")
    section_index = lax.axis_index("pipe")
    source = lax.axis_index("expert")
    micro_count, tok_rows, features = inputs.shape
    experts = router.shape[2]
    group_size = expert_width // experts
    tick_count = micro_count + sections - 1
    positions = jnp.arange(tok_rows, dtype=jnp.int32)
    slot_ids = jnp.arange(SLOT, dtype=jnp.int32)

    def expert_rows(received):
        row_shape = received.shape
        flat_rows = received.reshape(-1, row_shape[2])
        pre = lax.dot_general(
            flat_rows, w_up[0], (((1,), (1,)), ((), ())), preferred_element_type=jnp.float32
        )
        hidden = jax.nn.silu(pre).astype(jnp.bfloat16)
        partials = jnp.dot(hidden, w_down[0], preferred_element_type=jnp.float32).astype(
            jnp.bfloat16
        )
        return partials.reshape(row_shape)

    def layer(rows_in, micro_index):
        normed = rms_rows(rows_in)
        gate_values = jax.nn.sigmoid(jnp.dot(normed, router[0], preferred_element_type=jnp.float32))
        chosen = lax.dynamic_index_in_dim(picks[0], micro_index, 0, keepdims=False)
        local_rows = chosen - source * tok_rows
        owned = (local_rows >= 0) & (local_rows < tok_rows)
        owned_count = owned.astype(jnp.int32)
        slot_place = jnp.cumsum(owned_count, axis=1) - owned_count
        slot_hot = ((slot_place[:, :, None] == slot_ids) & owned[:, :, None]).astype(jnp.bfloat16)
        row_hot = (local_rows[:, :, None] == positions).astype(jnp.bfloat16)
        selector = jnp.einsum("ecr,ect->ert", slot_hot, row_hot, preferred_element_type=jnp.float32)
        picked = jnp.einsum(
            "ert,td->erd", selector.astype(jnp.bfloat16), normed, preferred_element_type=jnp.float32
        ).astype(jnp.bfloat16)
        copies = jnp.repeat(picked, group_size, axis=0)
        partials = expert_rows(
            lax.all_to_all(copies, "expert", split_axis=0, concat_axis=0, tiled=True)
        )
        returned = lax.all_to_all(partials, "expert", split_axis=0, concat_axis=0, tiled=True)
        expert_out = jnp.sum(
            returned.astype(jnp.float32).reshape(experts, group_size, SLOT, features), axis=1
        )
        weights = selector * jnp.transpose(gate_values)[:, None, :]
        update = jnp.einsum("ert,erd->td", weights, expert_out, precision=lax.Precision.HIGHEST)
        return (rows_in.astype(jnp.float32) + update).astype(jnp.bfloat16)

    def tick(tick_index, loop_state):
        previous, finals = loop_state
        arrived = passed_along(previous, "pipe", 1)
        micro_index = jnp.clip(tick_index - section_index, 0, micro_count - 1)
        fresh_rows = lax.dynamic_index_in_dim(
            inputs, jnp.clip(tick_index, 0, micro_count - 1), 0, keepdims=False
        )
        rows_in = jnp.where(section_index == 0, fresh_rows, arrived)
        result = layer(rows_in, micro_index)
        finished = (
            (section_index == sections - 1)
            & (tick_index - section_index >= 0)
            & (tick_index - section_index < micro_count)
        )
        stored = lax.dynamic_update_index_in_dim(finals, result, micro_index, 0)
        finals = jnp.where(finished, stored, finals)
        return (result, finals)

    start_rows = jnp.zeros((tok_rows, features), jnp.bfloat16)
    start_finals = jnp.zeros((micro_count, tok_rows, features), jnp.bfloat16)
    previous, finals = lax.fori_loop(0, tick_count, tick, (start_rows, start_finals))
    shared = from_root(finals, "pipe", sections - 1)
    final_normed = rms_rows(shared)
    student_rows = jnp.einsum(
        "mtd,jd->mtj", final_normed, probe[0], preferred_element_type=jnp.float32
    )
    return student_rows.astype(jnp.bfloat16)[None]


def solution(mesh):
    return jax.shard_map(
        shards,
        mesh=mesh,
        in_specs=(
            P(None, "expert", None),
            P("pipe", None, None),
            P("pipe", "expert", None),
            P("pipe", "expert", None),
            P("pipe", None, None, None),
            P("pipe", None, None),
        ),
        out_specs=P("pipe", None, "expert", None),
        check_vma=False,
    )
```

profile of v0, /device:TPU:0, one launch (start us, length us, event | category | flops | bytes accessed | tf_op | source)
XLA Modules:
  0.0 138.6 jit_solution(14568044816781589299)
XLA Ops:
  7.7 95.9 %while.21 = (s32[]{:T(128)}, bf16[32,5120]{1,0:T(8,128)(2,1)}, bf16[1,32,5120]{2,1,0:T(8,128)(2,1)}, pred[]{:T(512)}, bf16[1,32,5120]{2,1,0:T(8,128)(2,1)}, /*in...) while((s32[]{:T(128)}, bf16[32,5120]{1,0:T(8,128)(2,1)}, ...), condition=%wide.region_4.5_spmd.clone, body=%wide.region_1.4_spmd.clone.sunk | while | flops 71040296 | bytes 23656336 | solution.py:96
  7.7 5.0 %collective-permute-start = (bf16[32,5120]{1,0:T(8,128)(2,1)S(1)}, bf16[32,5120]{1,0:T(8,128)(2,1)S(1)}, u32[]{:S(2)}, u32[]{:S(2)}) collective-permute-start(bf16[32,5120]{1,0:T(8,128)(2,1)S(1)} %broadcast_select_fusion.3), channel_id=1, source_target_pairs={{0,16},{1,17},{2,18},{3,19},{4,20},{5,21},{6,22},{7,23},{8,24},{9,... | collective-permute-start | bytes 983048 | tf_op jit(solution)/shard_map/while/body/eval_jaxpr/ppermute | solution.py:12
  12.7 6.9 %collective-permute-done = bf16[32,5120]{1,0:T(8,128)(2,1)S(1)} collective-permute-done((bf16[32,5120]{1,0:T(8,128)(2,1)S(1)}, bf16[32,5120]{1,0:T(8,128)(2,1)S(1)}, u32[]{:S(2)}, u32[]{:S(2)}) %collective-permute-start) | collective-permute-done | bytes 327712 | tf_op jit(solution)/shard_map/while/body/eval_jaxpr/ppermute | solution.py:12
  19.7 1.2 fusion.64
  21.8 0.8 reduce.13
  22.6 14.2 %all_to_all.32 = bf16[16,2,2560]{2,1,0:T(2,128)(2,1)S(1)} all-to-all(bf16[16,2,2560]{2,1,0:T(2,128)(2,1)S(1)} %reshape.138), channel_id=1, replica_groups=mesh['pipe'=2,'expert'=16] {'expert'}, dimensions={0} | all-to-all | bytes 327680 | tf_op jit(solution)/shard_map/while/body/eval_jaxpr/all_to_all | solution.py:66
  37.0 3.0 %fusion.66 = bf16[16,1,5120]{2,0,1:T(8,128)(2,1)S(1)} fusion(bf16[1,192,5120]{2,1,0:T(8,128)(2,1)} %get-tuple-element.587, bf16[1,192,5120]{2,1,0:T(8,128)(2,1)S(1)} %copy-done.1, bf16[16,1,5120]{2,1,0:T(2,128)(2,1)S(1)} %reshape.139), kind=kOutput, calls=%fused_computation.3.clone.1 | convolution fusion | flops 63011840 | bytes 4259840 | tf_op jit(solution)/shard_map/while/body/eval_jaxpr/dot_general | solution.py:45
  42.1 3.5 %all-to-all-start.1 = ((bf16[16,2,2560]{2,1,0:T(2,128)(2,1)}), bf16[16,2,2560]{2,1,0:T(2,128)(2,1)S(1)}, u32[]{:S(2)}, u32[]{:S(2)}) async-start(bf16[16,2,2560]{2,1,0:T(2,128)(2,1)} %reshape.140), calls=%async_computation.1 | async-start | bytes 327680 | tf_op jit(solution)/shard_map/while/body/eval_jaxpr/all_to_all | solution.py:68
  45.9 8.1 %all-to-all-done.1 = bf16[16,2,2560]{2,1,0:T(2,128)(2,1)S(1)} async-done(((bf16[16,2,2560]{2,1,0:T(2,128)(2,1)}), bf16[16,2,2560]{2,1,0:T(2,128)(2,1)S(1)}, u32[]{:S(2)}, u32[]{:S(2)}) %all-to-all-start.1) | async-done | bytes 163872 | tf_op jit(solution)/shard_map/while/body/eval_jaxpr/all_to_all | solution.py:68
  54.7 1.6 %bitcast_select_fusion.4 = (bf16[1,32,5120]{2,1,0:T(8,128)(2,1)S(1)}, bf16[32,5120]{1,0:T(8,128)(2,1)}) fusion(bf16[1,32,5120]{2,1,0:T(8,128)(2,1)S(1)} %copy-done.2, pred[]{:T(512)S(6)} %compare.3, pred[]{:T(512)S(6)} %and.69, f32[2,32]{1,0:T(2,128)S(1)} %fusion.67, f32[2,5120]{1,0:T(2,128)S(1)} %bitcast_reduce_fusion.2, ...), kind=kOutput, calls=%fused_computation.20.clone.1 | convolution fusion | flops 4751360 | bytes 1351938 | tf_op jit(solution)/shard_map/while/body/eval_jaxpr/ert,erd->td/dot_general | solution.py:73
  57.0 1.1 broadcast_select_fusion.3
  58.1 4.4 %collective-permute-start = (bf16[32,5120]{1,0:T(8,128)(2,1)S(1)}, bf16[32,5120]{1,0:T(8,128)(2,1)S(1)}, u32[]{:S(2)}, u32[]{:S(2)}) collective-permute-start(bf16[32,5120]{1,0:T(8,128)(2,1)S(1)} %broadcast_select_fusion.3), channel_id=1, source_target_pairs={{0,16},{1,17},{2,18},{3,19},{4,20},{5,21},{6,22},{7,23},{8,24},{9,... | collective-permute-start | bytes 983048 | tf_op jit(solution)/shard_map/while/body/eval_jaxpr/ppermute | solution.py:12
  62.5 6.3 %collective-permute-done = bf16[32,5120]{1,0:T(8,128)(2,1)S(1)} collective-permute-done((bf16[32,5120]{1,0:T(8,128)(2,1)S(1)}, bf16[32,5120]{1,0:T(8,128)(2,1)S(1)}, u32[]{:S(2)}, u32[]{:S(2)}) %collective-permute-start) | collective-permute-done | bytes 327712 | tf_op jit(solution)/shard_map/while/body/eval_jaxpr/ppermute | solution.py:12
  68.9 1.2 fusion.64
  71.0 0.8 reduce.13
  71.8 11.6 %all_to_all.32 = bf16[16,2,2560]{2,1,0:T(2,128)(2,1)S(1)} all-to-all(bf16[16,2,2560]{2,1,0:T(2,128)(2,1)S(1)} %reshape.138), channel_id=1, replica_groups=mesh['pipe'=2,'expert'=16] {'expert'}, dimensions={0} | all-to-all | bytes 327680 | tf_op jit(solution)/shard_map/while/body/eval_jaxpr/all_to_all | solution.py:66
  83.6 3.0 %fusion.66 = bf16[16,1,5120]{2,0,1:T(8,128)(2,1)S(1)} fusion(bf16[1,192,5120]{2,1,0:T(8,128)(2,1)} %get-tuple-element.587, bf16[1,192,5120]{2,1,0:T(8,128)(2,1)S(1)} %copy-done.1, bf16[16,1,5120]{2,1,0:T(2,128)(2,1)S(1)} %reshape.139), kind=kOutput, calls=%fused_computation.3.clone.1 | convolution fusion | flops 63011840 | bytes 4259840 | tf_op jit(solution)/shard_map/while/body/eval_jaxpr/dot_general | solution.py:45
  87.2 0.8 reduce.14
  88.7 3.5 %all-to-all-start.1 = ((bf16[16,2,2560]{2,1,0:T(2,128)(2,1)}), bf16[16,2,2560]{2,1,0:T(2,128)(2,1)S(1)}, u32[]{:S(2)}, u32[]{:S(2)}) async-start(bf16[16,2,2560]{2,1,0:T(2,128)(2,1)} %reshape.140), calls=%async_computation.1 | async-start | bytes 327680 | tf_op jit(solution)/shard_map/while/body/eval_jaxpr/all_to_all | solution.py:68
  92.6 8.1 %all-to-all-done.1 = bf16[16,2,2560]{2,1,0:T(2,128)(2,1)S(1)} async-done(((bf16[16,2,2560]{2,1,0:T(2,128)(2,1)}), bf16[16,2,2560]{2,1,0:T(2,128)(2,1)S(1)}, u32[]{:S(2)}, u32[]{:S(2)}) %all-to-all-start.1) | async-done | bytes 163872 | tf_op jit(solution)/shard_map/while/body/eval_jaxpr/all_to_all | solution.py:68
  101.3 1.6 %bitcast_select_fusion.4 = (bf16[1,32,5120]{2,1,0:T(8,128)(2,1)S(1)}, bf16[32,5120]{1,0:T(8,128)(2,1)}) fusion(bf16[1,32,5120]{2,1,0:T(8,128)(2,1)S(1)} %copy-done.2, pred[]{:T(512)S(6)} %compare.3, pred[]{:T(512)S(6)} %and.69, f32[2,32]{1,0:T(2,128)S(1)} %fusion.67, f32[2,5120]{1,0:T(2,128)S(1)} %bitcast_reduce_fusion.2, ...), kind=kOutput, calls=%fused_computation.20.clone.1 | convolution fusion | flops 4751360 | bytes 1351938 | tf_op jit(solution)/shard_map/while/body/eval_jaxpr/ert,erd->td/dot_general | solution.py:73
  104.4 24.3 %all-reduce.2.cloned.1.call-done = bf16[1,32,5120]{2,1,0:T(8,128)(2,1)} async-done(((bf16[1,32,5120]{2,1,0:T(8,128)(2,1)}), bf16[1,32,5120]{2,1,0:T(8,128)(2,1)}) %all-reduce.2.cloned.1.call-update) | async-done | bytes 327696 | tf_op jit(solution)/shard_map/psum | solution.py:17
  128.6 1.1 fusion.29
  129.8 1.9 %fusion.28 = bf16[1,1,32,64]{3,2,1,0:T(8,128)(2,1)} fusion(bf16[1,64,5120]{2,1,0:T(8,128)(2,1)S(1)} %copy-done, bf16[1,32,5120]{2,1,0:T(8,128)(2,1)} %all-reduce.2.cloned.1.call-done, f32[32]{0:T(128)S(1)} %add_rsqrt_fusion.1), kind=kOutput, calls=%fused_computation.32 | convolution fusion | flops 21465088 | bytes 987264 | tf_op jit(solution)/shard_map/mtd,jd->mtj/dot_general | solution.py:99
  (55 shorter events, 10.9 us)
Async XLA Ops:
  6.5 123.3 %copy-start = (bf16[1,64,5120]{2,1,0:T(8,128)(2,1)S(1)}, bf16[1,64,5120]{2,1,0:T(8,128)(2,1)}, u32[]{:S(2)}) copy-start(bf16[1,64,5120]{2,1,0:T(8,128)(2,1)} %param.13) | copy-start | bytes 1966084
  6.5 122.1 %all-reduce.2.cloned.1.call-start = ((), (), s32[]{:S(2)}) async-start(), calls=%async_computation.2 | async-start | bytes 655360 | tf_op jit(solution)/shard_map/psum | solution.py:17
  7.7 29.3 %copy-start.1 = (bf16[1,192,5120]{2,1,0:T(8,128)(2,1)S(1)}, bf16[1,192,5120]{2,1,0:T(8,128)(2,1)}, u32[]{:S(2)}) copy-start(bf16[1,192,5120]{2,1,0:T(8,128)(2,1)} %get-tuple-element.586) | copy-start | bytes 5898244 | tf_op jit(solution)/shard_map/while
  7.7 12.0 %collective-permute-start = (bf16[32,5120]{1,0:T(8,128)(2,1)S(1)}, bf16[32,5120]{1,0:T(8,128)(2,1)S(1)}, u32[]{:S(2)}, u32[]{:S(2)}) collective-permute-start(bf16[32,5120]{1,0:T(8,128)(2,1)S(1)} %broadcast_select_fusion.3), channel_id=1, source_target_pairs={{0,16},{1,17},{2,18},{3,19},{4,20},{5,21},{6,22},{7,23},{8,24},{9,... | collective-permute-start | bytes 983048 | tf_op jit(solution)/shard_map/while/body/eval_jaxpr/ppermute | solution.py:12
  36.9 8.7 %copy-start.4 = (bf16[1,5120,2]{1,2,0:T(2,128)(2,1)S(1)}, bf16[1,5120,2]{1,2,0:T(2,128)(2,1)}, u32[]{:S(2)}) copy-start(bf16[1,5120,2]{1,2,0:T(2,128)(2,1)} %get-tuple-element.583) | copy-start | bytes 61444 | tf_op jit(solution)/shard_map/while
  40.0 14.7 %copy-start.2 = (bf16[1,32,5120]{2,1,0:T(8,128)(2,1)S(1)}, bf16[1,32,5120]{2,1,0:T(8,128)(2,1)}, u32[]{:S(2)}) copy-start(bf16[1,32,5120]{2,1,0:T(8,128)(2,1)} %get-tuple-element.564) | copy-start | bytes 983044 | tf_op jit(solution)/shard_map/while
  42.1 11.9 %all-to-all-start.1 = ((bf16[16,2,2560]{2,1,0:T(2,128)(2,1)}), bf16[16,2,2560]{2,1,0:T(2,128)(2,1)S(1)}, u32[]{:S(2)}, u32[]{:S(2)}) async-start(bf16[16,2,2560]{2,1,0:T(2,128)(2,1)} %reshape.140), calls=%async_computation.1 | async-start | bytes 327680 | tf_op jit(solution)/shard_map/while/body/eval_jaxpr/all_to_all | solution.py:68
  56.2 0.7 copy-start.3
  57.0 26.6 %copy-start.1 = (bf16[1,192,5120]{2,1,0:T(8,128)(2,1)S(1)}, bf16[1,192,5120]{2,1,0:T(8,128)(2,1)}, u32[]{:S(2)}) copy-start(bf16[1,192,5120]{2,1,0:T(8,128)(2,1)} %get-tuple-element.586) | copy-start | bytes 5898244 | tf_op jit(solution)/shard_map/while
  58.1 10.8 %collective-permute-start = (bf16[32,5120]{1,0:T(8,128)(2,1)S(1)}, bf16[32,5120]{1,0:T(8,128)(2,1)S(1)}, u32[]{:S(2)}, u32[]{:S(2)}) collective-permute-start(bf16[32,5120]{1,0:T(8,128)(2,1)S(1)} %broadcast_select_fusion.3), channel_id=1, source_target_pairs={{0,16},{1,17},{2,18},{3,19},{4,20},{5,21},{6,22},{7,23},{8,24},{9,... | collective-permute-start | bytes 983048 | tf_op jit(solution)/shard_map/while/body/eval_jaxpr/ppermute | solution.py:12
  83.6 8.7 %copy-start.4 = (bf16[1,5120,2]{1,2,0:T(2,128)(2,1)S(1)}, bf16[1,5120,2]{1,2,0:T(2,128)(2,1)}, u32[]{:S(2)}) copy-start(bf16[1,5120,2]{1,2,0:T(2,128)(2,1)} %get-tuple-element.583) | copy-start | bytes 61444 | tf_op jit(solution)/shard_map/while
  86.6 14.7 %copy-start.2 = (bf16[1,32,5120]{2,1,0:T(8,128)(2,1)S(1)}, bf16[1,32,5120]{2,1,0:T(8,128)(2,1)}, u32[]{:S(2)}) copy-start(bf16[1,32,5120]{2,1,0:T(8,128)(2,1)} %get-tuple-element.564) | copy-start | bytes 983044 | tf_op jit(solution)/shard_map/while
  88.7 11.9 %all-to-all-start.1 = ((bf16[16,2,2560]{2,1,0:T(2,128)(2,1)}), bf16[16,2,2560]{2,1,0:T(2,128)(2,1)S(1)}, u32[]{:S(2)}, u32[]{:S(2)}) async-start(bf16[16,2,2560]{2,1,0:T(2,128)(2,1)} %reshape.140), calls=%async_computation.1 | async-start | bytes 327680 | tf_op jit(solution)/shard_map/while/body/eval_jaxpr/all_to_all | solution.py:68
  102.9 0.7 copy-start.3
Sparse Core Ops, SparseCore 0:
  104.5 24.1 all-reduce.1
where the time goes:
time: 139 us
  waiting for transfers between devices  53.8 us (39%)
  blocking collectives  25.8 us (19%)
  starting transfers between devices  16.5 us (12%)
  between operations  13.4 us (10%)
  matrix products  12.4 us (9%)
  other arithmetic  10.4 us (7%)
  local copies, waits for them, and re-layouts  6.15 us (4%)
    all_to_all x2, blocking collectives, layer(): lax.all_to_all(copies, 'expert', split_axis=0, concat_axis=0, tiled=True)  25.8 us
    psum x1, waiting for transfers between devices, from_root(): return lax.psum(jnp.where(mine, x, jnp.zeros_like(x)), axis)  24.3 us
    all_to_all x2, waiting for transfers between devices, layer(): lax.all_to_all(partials, 'expert', split_axis=0, concat_axis=0, tiled=True)  16.2 us
    ppermute x2, waiting for transfers between devices, passed_along(): return lax.ppermute(x, axis, pairs)  13.3 us
    ppermute x2, starting transfers between devices, passed_along(): return lax.ppermute(x, axis, pairs)  9.43 us
    all_to_all x2, starting transfers between devices, layer(): lax.all_to_all(partials, 'expert', split_axis=0, concat_axis=0, tiled=True)  7.03 us
    dot_general x2, matrix products, expert_rows(): jnp.dot(hidden, w_down[0], preferred_element_type=jnp.float32)  6.05 us
    while x24, local copies, waits for them, and re-layouts  3.7 us
  transfers between devices with their start and end apart: 5, of which 5 were waited for; matrix products, arithmetic and copies ran while one was open for 0% of the time, Pallas kernels for 0%

commit v1 on v0

--- a/solution.py
+++ b/solution.py
@@ -4,6 +4,30 @@
 from jax.sharding import PartitionSpec as P
 
 SLOT = 1
+
+
+def cut_along(x, dim, size):
+    shape = x.shape
+    pieces = x.reshape(*shape[:dim], size, shape[dim] // size, *shape[dim + 1 :])
+    return jnp.moveaxis(pieces, dim, 0)
+
+
+def laid_out(blocks, dim):
+    blocks = jnp.moveaxis(blocks, 0, dim)
+    dims = blocks.shape
+    return blocks.reshape(*dims[:dim], dims[dim] * dims[dim + 1], *dims[dim + 2 :])
+
+
+def sent_to_each(array, axis, split_dim, concat_dim):
+    devices, index = (lax.axis_size(axis), lax.axis_index(axis))
+    pieces = cut_along(array, split_dim, devices)
+    out = pieces
+    for step in range(1, devices):
+        target, source = ((index + step) % devices, (index - step) % devices)
+        sent = lax.dynamic_index_in_dim(pieces, target, 0)
+        other = lax.ppermute(sent, axis, [(i, (i + step) % devices) for i in range(devices)])
+        out = lax.dynamic_update_slice_in_dim(out, other, source, axis=0)
+    return laid_out(out, concat_dim)
 
 
 def passed_along(x, axis, by):
@@ -62,9 +86,7 @@
             "ert,td->erd", selector.astype(jnp.bfloat16), normed, preferred_element_type=jnp.float32
         ).astype(jnp.bfloat16)
         copies = jnp.repeat(picked, group_size, axis=0)
-        partials = expert_rows(
-            lax.all_to_all(copies, "expert", split_axis=0, concat_axis=0, tiled=True)
-        )
+        partials = expert_rows(sent_to_each(copies, "expert", 0, 0))
         returned = lax.all_to_all(partials, "expert", split_axis=0, concat_axis=0, tiled=True)
         expert_out = jnp.sum(
             returned.astype(jnp.float32).reshape(experts, group_size, SLOT, features), axis=1

time: 139 us -> 160 us (1.15)
  starting transfers between devices: 16.5 us -> 57.4 us
  blocking collectives: 25.8 us -> 0 us
  local copies, waits for them, and re-layouts: 6.15 us -> 13.5 us
  other arithmetic: 10.4 us -> 7.52 us
  waiting for transfers between devices: 53.8 us -> 56 us
    ppermute x0 -> x30, starting transfers between devices: none -> 41.1 us  [sent_to_each(): lax.ppermute(sent, axis, [(i, (i + step) % devices) for i in range(device...]
    all_to_all x2 -> x0, blocking collectives: 25.8 us -> none  [layer(): lax.all_to_all(copies, 'expert', split_axis=0, concat_axis=0, tiled=True)]
    dynamic_update_slice x0 -> x30, local copies, waits for them, and re-layouts: none -> 8.48 us  [sent_to_each(): out = lax.dynamic_update_slice_in_dim(out, other, source, axis=0)]
    ppermute x0 -> x30, waiting for transfers between devices: none -> 2.67 us  [sent_to_each(): lax.ppermute(sent, axis, [(i, (i + step) % devices) for i in range(device...]
    while x24 -> x20, local copies, waits for them, and re-layouts: 3.7 us -> 3.23 us
  transfers between devices with their start and end apart: 5 -> 35, of which waited for: 5 -> 7; matrix products, arithmetic and copies ran while one was open for 0% -> 5% of each run, Pallas kernels for 0% -> 0%
where the time goes in v1:
time: 160 us
  starting transfers between devices  57.4 us (36%)
  waiting for transfers between devices  56 us (35%)
  local copies, waits for them, and re-layouts  13.5 us (8%)
  between operations  13.4 us (8%)
  matrix products  11 us (7%)
  other arithmetic  7.52 us (5%)
    ppermute x30, starting transfers between devices, sent_to_each(): lax.ppermute(sent, axis, [(i, (i + step) % devices) for i in range(device...  41.1 us
    psum x1, waiting for transfers between devices, from_root(): return lax.psum(jnp.where(mine, x, jnp.zeros_like(x)), axis)  24.3 us
    all_to_all x2, waiting for transfers between devices, layer(): lax.all_to_all(partials, 'expert', split_axis=0, concat_axis=0, tiled=True)  16.2 us
    ppermute x2, waiting for transfers between devices, passed_along(): return lax.ppermute(x, axis, pairs)  12.8 us
    ppermute x2, starting transfers between devices, passed_along(): return lax.ppermute(x, axis, pairs)  9.29 us
    dynamic_update_slice x30, local copies, waits for them, and re-layouts, sent_to_each(): out = lax.dynamic_update_slice_in_dim(out, other, source, axis=0)  8.48 us
    all_to_all x2, starting transfers between devices, layer(): lax.all_to_all(partials, 'expert', split_axis=0, concat_axis=0, tiled=True)  7.03 us
    dot_general x2, matrix products, expert_rows(): jnp.dot(hidden, w_down[0], preferred_element_type=jnp.float32)  6.05 us
  transfers between devices with their start and end apart: 35, of which 7 were waited for; matrix products, arithmetic and copies ran while one was open for 5% of the time, Pallas kernels for 0%

profile of v1, /device:TPU:0, one launch (start us, length us, event | category | flops | bytes accessed | tf_op | source)
XLA Modules:
  0.0 159.9 jit_solution(3570342257433782002)
XLA Ops:
  7.7 117.2 %while.21 = (s32[]{:T(128)}, bf16[32,5120]{1,0:T(8,128)(2,1)S(1)}, bf16[1,32,5120]{2,1,0:T(8,128)(2,1)}, pred[]{:T(512)}, bf16[1,32,5120]{2,1,0:T(8,128)(2,1)}, ...) while((s32[]{:T(128)}, bf16[32,5120]{1,0:T(8,128)(2,1)S(1)}, ...), condition=%wide.region_4.5_spmd.clone, body=%wide.region_1.4_spmd.clone.sunk | while | flops 71040752 | bytes 23743880 | solution.py:118
  7.7 4.9 %collective-permute-start = (bf16[32,5120]{1,0:T(8,128)(2,1)S(1)}, bf16[32,5120]{1,0:T(8,128)(2,1)S(1)}, u32[]{:S(2)}, u32[]{:S(2)}) collective-permute-start(bf16[32,5120]{1,0:T(8,128)(2,1)S(1)} %broadcast_select_fusion.3), channel_id=1, source_target_pairs={{0,16},{1,17},{2,18},{3,19},{4,20},{5,21},{6,22},{7,23},{8,24},{9,... | collective-permute-start | bytes 983048 | tf_op jit(solution)/shard_map/while/body/eval_jaxpr/ppermute | solution.py:36
  12.8 6.7 %collective-permute-done = bf16[32,5120]{1,0:T(8,128)(2,1)S(1)} collective-permute-done((bf16[32,5120]{1,0:T(8,128)(2,1)S(1)}, bf16[32,5120]{1,0:T(8,128)(2,1)S(1)}, u32[]{:S(2)}, u32[]{:S(2)}) %collective-permute-start) | collective-permute-done | bytes 327712 | tf_op jit(solution)/shard_map/while/body/eval_jaxpr/ppermute | solution.py:36
  23.1 2.4 %collective-permute-start.3 = (bf16[1,1,1,5120]{3,0,2,1:T(2,128)(2,1)S(1)}, bf16[1,1,1,5120]{3,0,2,1:T(2,128)(2,1)S(1)}, u32[]{:S(2)}, u32[]{:S(2)}) collective-permute-start(bf16[1,1,1,5120]{3,0,2,1:T(2,128)(2,1)S(1)} %get-tuple-element.610), channel_id=1, source_target_pairs={{0,3},{1,4},{2,5},{3,6},{4,7},{5,8},{6,9},{7,10},{8,11},{9,12},{10... | collective-permute-start | bytes 30728 | tf_op jit(solution)/shard_map/while/body/eval_jaxpr/ppermute | solution.py:28
  28.4 4.3 %collective-permute-start.7 = (bf16[1,1,1,5120]{3,0,2,1:T(2,128)(2,1)S(1)}, bf16[1,1,1,5120]{3,0,2,1:T(2,128)(2,1)S(1)}, u32[]{:S(2)}, u32[]{:S(2)}) collective-permute-start(bf16[1,1,1,5120]{3,0,2,1:T(2,128)(2,1)S(1)} %get-tuple-element.614), channel_id=1, source_target_pairs={{0,7},{1,8},{2,9},{3,10},{4,11},{5,12},{6,13},{7,14},{8,15},{9,0},... | collective-permute-start | bytes 30728 | tf_op jit(solution)/shard_map/while/body/eval_jaxpr/ppermute | solution.py:28
  33.4 2.4 %collective-permute-start.10 = (bf16[1,1,1,5120]{3,0,2,1:T(2,128)(2,1)S(1)}, bf16[1,1,1,5120]{3,0,2,1:T(2,128)(2,1)S(1)}, u32[]{:S(2)}, u32[]{:S(2)}) collective-permute-start(bf16[1,1,1,5120]{3,0,2,1:T(2,128)(2,1)S(1)} %get-tuple-element.617), channel_id=1, source_target_pairs={{0,10},{1,11},{2,12},{3,13},{4,14},{5,15},{6,0},{7,1},{8,2},{9,3},... | collective-permute-start | bytes 30728 | tf_op jit(solution)/shard_map/while/body/eval_jaxpr/ppermute | solution.py:28
  35.8 2.9 %collective-permute-start.11 = (bf16[1,1,1,5120]{3,0,2,1:T(2,128)(2,1)S(1)}, bf16[1,1,1,5120]{3,0,2,1:T(2,128)(2,1)S(1)}, u32[]{:S(2)}, u32[]{:S(2)}) collective-permute-start(bf16[1,1,1,5120]{3,0,2,1:T(2,128)(2,1)S(1)} %get-tuple-element.618), channel_id=1, source_target_pairs={{0,11},{1,12},{2,13},{3,14},{4,15},{5,0},{6,1},{7,2},{8,3},{9,4},{... | collective-permute-start | bytes 30728 | tf_op jit(solution)/shard_map/while/body/eval_jaxpr/ppermute | solution.py:28
  38.7 1.8 %collective-permute-start.12 = (bf16[1,1,1,5120]{3,0,2,1:T(2,128)(2,1)S(1)}, bf16[1,1,1,5120]{3,0,2,1:T(2,128)(2,1)S(1)}, u32[]{:S(2)}, u32[]{:S(2)}) collective-permute-start(bf16[1,1,1,5120]{3,0,2,1:T(2,128)(2,1)S(1)} %get-tuple-element.619), channel_id=1, source_target_pairs={{0,12},{1,13},{2,14},{3,15},{4,0},{5,1},{6,2},{7,3},{8,4},{9,5},{1... | collective-permute-start | bytes 30728 | tf_op jit(solution)/shard_map/while/body/eval_jaxpr/ppermute | solution.py:28
  42.0 2.2 %collective-permute-start.15 = (bf16[1,1,1,5120]{3,0,2,1:T(2,128)(2,1)S(1)}, bf16[1,1,1,5120]{3,0,2,1:T(2,128)(2,1)S(1)}, u32[]{:S(2)}, u32[]{:S(2)}) collective-permute-start(bf16[1,1,1,5120]{3,0,2,1:T(2,128)(2,1)S(1)} %get-tuple-element.622), channel_id=1, source_target_pairs={{0,15},{1,0},{2,1},{3,2},{4,3},{5,4},{6,5},{7,6},{8,7},{9,8},{10,9... | collective-permute-start | bytes 30728 | tf_op jit(solution)/shard_map/while/body/eval_jaxpr/ppermute | solution.py:28
  48.6 3.0 %fusion.61 = bf16[16,1,5120]{2,0,1:T(8,128)(2,1)S(1)} fusion(bf16[1,192,5120]{2,1,0:T(8,128)(2,1)} %get-tuple-element.726, bf16[16,5120]{1,0:T(8,128)(2,1)S(1)} %dynamic_update_slice.258, bf16[1,192,5120]{2,1,0:T(8,128)(2,1)S(1)} %copy-done.1), kind=kOutput, calls=%fused_computation.3.clone.1 | convolution fusion | flops 63011840 | bytes 4259840 | tf_op jit(solution)/shard_map/while/body/eval_jaxpr/dot_general | solution.py:69
  53.5 3.5 %all-to-all-start = ((bf16[16,2,2560]{2,1,0:T(2,128)(2,1)}), bf16[16,2,2560]{2,1,0:T(2,128)(2,1)S(1)}, u32[]{:S(2)}, u32[]{:S(2)}) async-start(bf16[16,2,2560]{2,1,0:T(2,128)(2,1)} %reshape.335), calls=%async_computation | async-start | bytes 327680 | tf_op jit(solution)/shard_map/while/body/eval_jaxpr/all_to_all | solution.py:90
  57.3 8.1 %all-to-all-done = bf16[16,2,2560]{2,1,0:T(2,128)(2,1)S(1)} async-done(((bf16[16,2,2560]{2,1,0:T(2,128)(2,1)}), bf16[16,2,2560]{2,1,0:T(2,128)(2,1)S(1)}, u32[]{:S(2)}, u32[]{:S(2)}) %all-to-all-start) | async-done | bytes 163872 | tf_op jit(solution)/shard_map/while/body/eval_jaxpr/all_to_all | solution.py:90
  67.7 4.4 %collective-permute-start = (bf16[32,5120]{1,0:T(8,128)(2,1)S(1)}, bf16[32,5120]{1,0:T(8,128)(2,1)S(1)}, u32[]{:S(2)}, u32[]{:S(2)}) collective-permute-start(bf16[32,5120]{1,0:T(8,128)(2,1)S(1)} %broadcast_select_fusion.3), channel_id=1, source_target_pairs={{0,16},{1,17},{2,18},{3,19},{4,20},{5,21},{6,22},{7,23},{8,24},{9,... | collective-permute-start | bytes 983048 | tf_op jit(solution)/shard_map/while/body/eval_jaxpr/ppermute | solution.py:36
  72.3 6.1 %collective-permute-done = bf16[32,5120]{1,0:T(8,128)(2,1)S(1)} collective-permute-done((bf16[32,5120]{1,0:T(8,128)(2,1)S(1)}, bf16[32,5120]{1,0:T(8,128)(2,1)S(1)}, u32[]{:S(2)}, u32[]{:S(2)}) %collective-permute-start) | collective-permute-done | bytes 327712 | tf_op jit(solution)/shard_map/while/body/eval_jaxpr/ppermute | solution.py:36
  83.8 2.5 %collective-permute-done.1 = bf16[1,1,1,5120]{3,0,2,1:T(2,128)(2,1)S(1)} collective-permute-done((bf16[1,1,1,5120]{3,0,2,1:T(2,128)(2,1)S(1)}, bf16[1,1,1,5120]{3,0,2,1:T(2,128)(2,1)S(1)}, u32[]{:S(2)}, u32[]{:S(2)}) %collective-permute-start.1) | collective-permute-done | bytes 10272 | tf_op jit(solution)/shard_map/while/body/eval_jaxpr/ppermute | solution.py:28
  87.1 2.6 %collective-permute-start.7 = (bf16[1,1,1,5120]{3,0,2,1:T(2,128)(2,1)S(1)}, bf16[1,1,1,5120]{3,0,2,1:T(2,128)(2,1)S(1)}, u32[]{:S(2)}, u32[]{:S(2)}) collective-permute-start(bf16[1,1,1,5120]{3,0,2,1:T(2,128)(2,1)S(1)} %get-tuple-element.614), channel_id=1, source_target_pairs={{0,7},{1,8},{2,9},{3,10},{4,11},{5,12},{6,13},{7,14},{8,15},{9,0},... | collective-permute-start | bytes 30728 | tf_op jit(solution)/shard_map/while/body/eval_jaxpr/ppermute | solution.py:28
  91.3 1.8 %collective-permute-start.10 = (bf16[1,1,1,5120]{3,0,2,1:T(2,128)(2,1)S(1)}, bf16[1,1,1,5120]{3,0,2,1:T(2,128)(2,1)S(1)}, u32[]{:S(2)}, u32[]{:S(2)}) collective-permute-start(bf16[1,1,1,5120]{3,0,2,1:T(2,128)(2,1)S(1)} %get-tuple-element.617), channel_id=1, source_target_pairs={{0,10},{1,11},{2,12},{3,13},{4,14},{5,15},{6,0},{7,1},{8,2},{9,3},... | collective-permute-start | bytes 30728 | tf_op jit(solution)/shard_map/while/body/eval_jaxpr/ppermute | solution.py:28
  93.1 3.6 %collective-permute-start.11 = (bf16[1,1,1,5120]{3,0,2,1:T(2,128)(2,1)S(1)}, bf16[1,1,1,5120]{3,0,2,1:T(2,128)(2,1)S(1)}, u32[]{:S(2)}, u32[]{:S(2)}) collective-permute-start(bf16[1,1,1,5120]{3,0,2,1:T(2,128)(2,1)S(1)} %get-tuple-element.618), channel_id=1, source_target_pairs={{0,11},{1,12},{2,13},{3,14},{4,15},{5,0},{6,1},{7,2},{8,3},{9,4},{... | collective-permute-start | bytes 30728 | tf_op jit(solution)/shard_map/while/body/eval_jaxpr/ppermute | solution.py:28
  99.4 2.0 %collective-permute-start.15 = (bf16[1,1,1,5120]{3,0,2,1:T(2,128)(2,1)S(1)}, bf16[1,1,1,5120]{3,0,2,1:T(2,128)(2,1)S(1)}, u32[]{:S(2)}, u32[]{:S(2)}) collective-permute-start(bf16[1,1,1,5120]{3,0,2,1:T(2,128)(2,1)S(1)} %get-tuple-element.622), channel_id=1, source_target_pairs={{0,15},{1,0},{2,1},{3,2},{4,3},{5,4},{6,5},{7,6},{8,7},{9,8},{10,9... | collective-permute-start | bytes 30728 | tf_op jit(solution)/shard_map/while/body/eval_jaxpr/ppermute | solution.py:28
  105.8 3.0 %fusion.61 = bf16[16,1,5120]{2,0,1:T(8,128)(2,1)S(1)} fusion(bf16[1,192,5120]{2,1,0:T(8,128)(2,1)} %get-tuple-element.726, bf16[16,5120]{1,0:T(8,128)(2,1)S(1)} %dynamic_update_slice.258, bf16[1,192,5120]{2,1,0:T(8,128)(2,1)S(1)} %copy-done.1), kind=kOutput, calls=%fused_computation.3.clone.1 | convolution fusion | flops 63011840 | bytes 4259840 | tf_op jit(solution)/shard_map/while/body/eval_jaxpr/dot_general | solution.py:69
  110.7 3.5 %all-to-all-start = ((bf16[16,2,2560]{2,1,0:T(2,128)(2,1)}), bf16[16,2,2560]{2,1,0:T(2,128)(2,1)S(1)}, u32[]{:S(2)}, u32[]{:S(2)}) async-start(bf16[16,2,2560]{2,1,0:T(2,128)(2,1)} %reshape.335), calls=%async_computation | async-start | bytes 327680 | tf_op jit(solution)/shard_map/while/body/eval_jaxpr/all_to_all | solution.py:90
  114.6 8.1 %all-to-all-done = bf16[16,2,2560]{2,1,0:T(2,128)(2,1)S(1)} async-done(((bf16[16,2,2560]{2,1,0:T(2,128)(2,1)}), bf16[16,2,2560]{2,1,0:T(2,128)(2,1)S(1)}, u32[]{:S(2)}, u32[]{:S(2)}) %all-to-all-start) | async-done | bytes 163872 | tf_op jit(solution)/shard_map/while/body/eval_jaxpr/all_to_all | solution.py:90
  125.7 24.3 %all-reduce.2.cloned.1.call-done = bf16[1,32,5120]{2,1,0:T(8,128)(2,1)} async-done(((bf16[1,32,5120]{2,1,0:T(8,128)(2,1)}), bf16[1,32,5120]{2,1,0:T(8,128)(2,1)}) %all-reduce.2.cloned.1.call-update) | async-done | bytes 327696 | tf_op jit(solution)/shard_map/psum | solution.py:41
  151.1 1.9 %fusion.22 = bf16[1,1,32,64]{3,2,1,0:T(8,128)(2,1)} fusion(bf16[1,64,5120]{2,1,0:T(8,128)(2,1)S(1)} %copy-done, bf16[1,32,5120]{2,1,0:T(8,128)(2,1)} %all-reduce.2.cloned.1.call-done, f32[32]{0:T(128)S(1)} %add_rsqrt_fusion.1), kind=kOutput, calls=%fused_computation.46 | convolution fusion | flops 21465088 | bytes 987264 | tf_op jit(solution)/shard_map/mtd,jd->mtj/dot_general | solution.py:121
  (137 shorter events, 39.3 us)
Async XLA Ops:
  6.5 143.4 %all-reduce.2.cloned.1.call-start = ((), (), s32[]{:S(2)}) async-start(), calls=%async_computation.1 | async-start | bytes 655360 | tf_op jit(solution)/shard_map/psum | solution.py:41
  7.7 11.8 %collective-permute-start = (bf16[32,5120]{1,0:T(8,128)(2,1)S(1)}, bf16[32,5120]{1,0:T(8,128)(2,1)S(1)}, u32[]{:S(2)}, u32[]{:S(2)}) collective-permute-start(bf16[32,5120]{1,0:T(8,128)(2,1)S(1)} %broadcast_select_fusion.3), channel_id=1, source_target_pairs={{0,16},{1,17},{2,18},{3,19},{4,20},{5,21},{6,22},{7,23},{8,24},{9,... | collective-permute-start | bytes 983048 | tf_op jit(solution)/shard_map/while/body/eval_jaxpr/ppermute | solution.py:36
  23.1 9.7 %collective-permute-start.3 = (bf16[1,1,1,5120]{3,0,2,1:T(2,128)(2,1)S(1)}, bf16[1,1,1,5120]{3,0,2,1:T(2,128)(2,1)S(1)}, u32[]{:S(2)}, u32[]{:S(2)}) collective-permute-start(bf16[1,1,1,5120]{3,0,2,1:T(2,128)(2,1)S(1)} %get-tuple-element.610), channel_id=1, source_target_pairs={{0,3},{1,4},{2,5},{3,6},{4,7},{5,8},{6,9},{7,10},{8,11},{9,12},{10... | collective-permute-start | bytes 30728 | tf_op jit(solution)/shard_map/while/body/eval_jaxpr/ppermute | solution.py:28
  25.5 7.6 %collective-permute-start.4 = (bf16[1,1,1,5120]{3,0,2,1:T(2,128)(2,1)S(1)}, bf16[1,1,1,5120]{3,0,2,1:T(2,128)(2,1)S(1)}, u32[]{:S(2)}, u32[]{:S(2)}) collective-permute-start(bf16[1,1,1,5120]{3,0,2,1:T(2,128)(2,1)S(1)} %get-tuple-element.611), channel_id=1, source_target_pairs={{0,4},{1,5},{2,6},{3,7},{4,8},{5,9},{6,10},{7,11},{8,12},{9,13},{1... | collective-permute-start | bytes 30728 | tf_op jit(solution)/shard_map/while/body/eval_jaxpr/ppermute | solution.py:28
  27.4 8.4 %collective-permute-start.6 = (bf16[1,1,1,5120]{3,0,2,1:T(2,128)(2,1)S(1)}, bf16[1,1,1,5120]{3,0,2,1:T(2,128)(2,1)S(1)}, u32[]{:S(2)}, u32[]{:S(2)}) collective-permute-start(bf16[1,1,1,5120]{3,0,2,1:T(2,128)(2,1)S(1)} %get-tuple-element.613), channel_id=1, source_target_pairs={{0,6},{1,7},{2,8},{3,9},{4,10},{5,11},{6,12},{7,13},{8,14},{9,15},... | collective-permute-start | bytes 30728 | tf_op jit(solution)/shard_map/while/body/eval_jaxpr/ppermute | solution.py:28
  28.4 10.2 %collective-permute-start.7 = (bf16[1,1,1,5120]{3,0,2,1:T(2,128)(2,1)S(1)}, bf16[1,1,1,5120]{3,0,2,1:T(2,128)(2,1)S(1)}, u32[]{:S(2)}, u32[]{:S(2)}) collective-permute-start(bf16[1,1,1,5120]{3,0,2,1:T(2,128)(2,1)S(1)} %get-tuple-element.614), channel_id=1, source_target_pairs={{0,7},{1,8},{2,9},{3,10},{4,11},{5,12},{6,13},{7,14},{8,15},{9,0},... | collective-permute-start | bytes 30728 | tf_op jit(solution)/shard_map/while/body/eval_jaxpr/ppermute | solution.py:28
  32.8 7.7 %collective-permute-start.8 = (bf16[1,1,1,5120]{3,0,2,1:T(2,128)(2,1)S(1)}, bf16[1,1,1,5120]{3,0,2,1:T(2,128)(2,1)S(1)}, u32[]{:S(2)}, u32[]{:S(2)}) collective-permute-start(bf16[1,1,1,5120]{3,0,2,1:T(2,128)(2,1)S(1)} %get-tuple-element.615), channel_id=1, source_target_pairs={{0,8},{1,9},{2,10},{3,11},{4,12},{5,13},{6,14},{7,15},{8,0},{9,1},... | collective-permute-start | bytes 30728 | tf_op jit(solution)/shard_map/while/body/eval_jaxpr/ppermute | solution.py:28
  33.1 7.4 %collective-permute-start.9 = (bf16[1,1,1,5120]{3,0,2,1:T(2,128)(2,1)S(1)}, bf16[1,1,1,5120]{3,0,2,1:T(2,128)(2,1)S(1)}, u32[]{:S(2)}, u32[]{:S(2)}) collective-permute-start(bf16[1,1,1,5120]{3,0,2,1:T(2,128)(2,1)S(1)} %get-tuple-element.616), channel_id=1, source_target_pairs={{0,9},{1,10},{2,11},{3,12},{4,13},{5,14},{6,15},{7,0},{8,1},{9,2},... | collective-permute-start | bytes 30728 | tf_op jit(solution)/shard_map/while/body/eval_jaxpr/ppermute | solution.py:28
  33.4 8.6 %collective-permute-start.10 = (bf16[1,1,1,5120]{3,0,2,1:T(2,128)(2,1)S(1)}, bf16[1,1,1,5120]{3,0,2,1:T(2,128)(2,1)S(1)}, u32[]{:S(2)}, u32[]{:S(2)}) collective-permute-start(bf16[1,1,1,5120]{3,0,2,1:T(2,128)(2,1)S(1)} %get-tuple-element.617), channel_id=1, source_target_pairs={{0,10},{1,11},{2,12},{3,13},{4,14},{5,15},{6,0},{7,1},{8,2},{9,3},... | collective-permute-start | bytes 30728 | tf_op jit(solution)/shard_map/while/body/eval_jaxpr/ppermute | solution.py:28
  35.8 11.2 %collective-permute-start.11 = (bf16[1,1,1,5120]{3,0,2,1:T(2,128)(2,1)S(1)}, bf16[1,1,1,5120]{3,0,2,1:T(2,128)(2,1)S(1)}, u32[]{:S(2)}, u32[]{:S(2)}) collective-permute-start(bf16[1,1,1,5120]{3,0,2,1:T(2,128)(2,1)S(1)} %get-tuple-element.618), channel_id=1, source_target_pairs={{0,11},{1,12},{2,13},{3,14},{4,15},{5,0},{6,1},{7,2},{8,3},{9,4},{... | collective-permute-start | bytes 30728 | tf_op jit(solution)/shard_map/while/body/eval_jaxpr/ppermute | solution.py:28
  38.7 8.7 %collective-permute-start.12 = (bf16[1,1,1,5120]{3,0,2,1:T(2,128)(2,1)S(1)}, bf16[1,1,1,5120]{3,0,2,1:T(2,128)(2,1)S(1)}, u32[]{:S(2)}, u32[]{:S(2)}) collective-permute-start(bf16[1,1,1,5120]{3,0,2,1:T(2,128)(2,1)S(1)} %get-tuple-element.619), channel_id=1, source_target_pairs={{0,12},{1,13},{2,14},{3,15},{4,0},{5,1},{6,2},{7,3},{8,4},{9,5},{1... | collective-permute-start | bytes 30728 | tf_op jit(solution)/shard_map/while/body/eval_jaxpr/ppermute | solution.py:28
  40.5 7.5 %collective-permute-start.14 = (bf16[1,1,1,5120]{3,0,2,1:T(2,128)(2,1)S(1)}, bf16[1,1,1,5120]{3,0,2,1:T(2,128)(2,1)S(1)}, u32[]{:S(2)}, u32[]{:S(2)}) collective-permute-start(bf16[1,1,1,5120]{3,0,2,1:T(2,128)(2,1)S(1)} %get-tuple-element.621), channel_id=1, source_target_pairs={{0,14},{1,15},{2,0},{3,1},{4,2},{5,3},{6,4},{7,5},{8,6},{9,7},{10,... | collective-permute-start | bytes 30728 | tf_op jit(solution)/shard_map/while/body/eval_jaxpr/ppermute | solution.py:28
  53.5 11.9 %all-to-all-start = ((bf16[16,2,2560]{2,1,0:T(2,128)(2,1)}), bf16[16,2,2560]{2,1,0:T(2,128)(2,1)S(1)}, u32[]{:S(2)}, u32[]{:S(2)}) async-start(bf16[16,2,2560]{2,1,0:T(2,128)(2,1)} %reshape.335), calls=%async_computation | async-start | bytes 327680 | tf_op jit(solution)/shard_map/while/body/eval_jaxpr/all_to_all | solution.py:90
  67.7 10.8 %collective-permute-start = (bf16[32,5120]{1,0:T(8,128)(2,1)S(1)}, bf16[32,5120]{1,0:T(8,128)(2,1)S(1)}, u32[]{:S(2)}, u32[]{:S(2)}) collective-permute-start(bf16[32,5120]{1,0:T(8,128)(2,1)S(1)} %broadcast_select_fusion.3), channel_id=1, source_target_pairs={{0,16},{1,17},{2,18},{3,19},{4,20},{5,21},{6,22},{7,23},{8,24},{9,... | collective-permute-start | bytes 983048 | tf_op jit(solution)/shard_map/while/body/eval_jaxpr/ppermute | solution.py:36
  81.1 8.6 %collective-permute-start.3 = (bf16[1,1,1,5120]{3,0,2,1:T(2,128)(2,1)S(1)}, bf16[1,1,1,5120]{3,0,2,1:T(2,128)(2,1)S(1)}, u32[]{:S(2)}, u32[]{:S(2)}) collective-permute-start(bf16[1,1,1,5120]{3,0,2,1:T(2,128)(2,1)S(1)} %get-tuple-element.610), channel_id=1, source_target_pairs={{0,3},{1,4},{2,5},{3,6},{4,7},{5,8},{6,9},{7,10},{8,11},{9,12},{10... | collective-permute-start | bytes 30728 | tf_op jit(solution)/shard_map/while/body/eval_jaxpr/ppermute | solution.py:28
  82.9 8.4 %collective-permute-start.4 = (bf16[1,1,1,5120]{3,0,2,1:T(2,128)(2,1)S(1)}, bf16[1,1,1,5120]{3,0,2,1:T(2,128)(2,1)S(1)}, u32[]{:S(2)}, u32[]{:S(2)}) collective-permute-start(bf16[1,1,1,5120]{3,0,2,1:T(2,128)(2,1)S(1)} %get-tuple-element.611), channel_id=1, source_target_pairs={{0,4},{1,5},{2,6},{3,7},{4,8},{5,9},{6,10},{7,11},{8,12},{9,13},{1... | collective-permute-start | bytes 30728 | tf_op jit(solution)/shard_map/while/body/eval_jaxpr/ppermute | solution.py:28
  83.5 7.8 %collective-permute-start.5 = (bf16[1,1,1,5120]{3,0,2,1:T(2,128)(2,1)S(1)}, bf16[1,1,1,5120]{3,0,2,1:T(2,128)(2,1)S(1)}, u32[]{:S(2)}, u32[]{:S(2)}) collective-permute-start(bf16[1,1,1,5120]{3,0,2,1:T(2,128)(2,1)S(1)} %get-tuple-element.612), channel_id=1, source_target_pairs={{0,5},{1,6},{2,7},{3,8},{4,9},{5,10},{6,11},{7,12},{8,13},{9,14},{... | collective-permute-start | bytes 30728 | tf_op jit(solution)/shard_map/while/body/eval_jaxpr/ppermute | solution.py:28
  87.1 9.6 %collective-permute-start.7 = (bf16[1,1,1,5120]{3,0,2,1:T(2,128)(2,1)S(1)}, bf16[1,1,1,5120]{3,0,2,1:T(2,128)(2,1)S(1)}, u32[]{:S(2)}, u32[]{:S(2)}) collective-permute-start(bf16[1,1,1,5120]{3,0,2,1:T(2,128)(2,1)S(1)} %get-tuple-element.614), channel_id=1, source_target_pairs={{0,7},{1,8},{2,9},{3,10},{4,11},{5,12},{6,13},{7,14},{8,15},{9,0},... | collective-permute-start | bytes 30728 | tf_op jit(solution)/shard_map/while/body/eval_jaxpr/ppermute | solution.py:28
  91.3 8.1 %collective-permute-start.10 = (bf16[1,1,1,5120]{3,0,2,1:T(2,128)(2,1)S(1)}, bf16[1,1,1,5120]{3,0,2,1:T(2,128)(2,1)S(1)}, u32[]{:S(2)}, u32[]{:S(2)}) collective-permute-start(bf16[1,1,1,5120]{3,0,2,1:T(2,128)(2,1)S(1)} %get-tuple-element.617), channel_id=1, source_target_pairs={{0,10},{1,11},{2,12},{3,13},{4,14},{5,15},{6,0},{7,1},{8,2},{9,3},... | collective-permute-start | bytes 30728 | tf_op jit(solution)/shard_map/while/body/eval_jaxpr/ppermute | solution.py:28
  93.1 11.2 %collective-permute-start.11 = (bf16[1,1,1,5120]{3,0,2,1:T(2,128)(2,1)S(1)}, bf16[1,1,1,5120]{3,0,2,1:T(2,128)(2,1)S(1)}, u32[]{:S(2)}, u32[]{:S(2)}) collective-permute-start(bf16[1,1,1,5120]{3,0,2,1:T(2,128)(2,1)S(1)} %get-tuple-element.618), channel_id=1, source_target_pairs={{0,11},{1,12},{2,13},{3,14},{4,15},{5,0},{6,1},{7,2},{8,3},{9,4},{... | collective-permute-start | bytes 30728 | tf_op jit(solution)/shard_map/while/body/eval_jaxpr/ppermute | solution.py:28
  96.7 7.9 %collective-permute-start.12 = (bf16[1,1,1,5120]{3,0,2,1:T(2,128)(2,1)S(1)}, bf16[1,1,1,5120]{3,0,2,1:T(2,128)(2,1)S(1)}, u32[]{:S(2)}, u32[]{:S(2)}) collective-permute-start(bf16[1,1,1,5120]{3,0,2,1:T(2,128)(2,1)S(1)} %get-tuple-element.619), channel_id=1, source_target_pairs={{0,12},{1,13},{2,14},{3,15},{4,0},{5,1},{6,2},{7,3},{8,4},{9,5},{1... | collective-permute-start | bytes 30728 | tf_op jit(solution)/shard_map/while/body/eval_jaxpr/ppermute | solution.py:28
  96.8 8.1 %collective-permute-start.13 = (bf16[1,1,1,5120]{3,0,2,1:T(2,128)(2,1)S(1)}, bf16[1,1,1,5120]{3,0,2,1:T(2,128)(2,1)S(1)}, u32[]{:S(2)}, u32[]{:S(2)}) collective-permute-start(bf16[1,1,1,5120]{3,0,2,1:T(2,128)(2,1)S(1)} %get-tuple-element.620), channel_id=1, source_target_pairs={{0,13},{1,14},{2,15},{3,0},{4,1},{5,2},{6,3},{7,4},{8,5},{9,6},{10... | collective-permute-start | bytes 30728 | tf_op jit(solution)/shard_map/while/body/eval_jaxpr/ppermute | solution.py:28
  97.9 7.3 %collective-permute-start.14 = (bf16[1,1,1,5120]{3,0,2,1:T(2,128)(2,1)S(1)}, bf16[1,1,1,5120]{3,0,2,1:T(2,128)(2,1)S(1)}, u32[]{:S(2)}, u32[]{:S(2)}) collective-permute-start(bf16[1,1,1,5120]{3,0,2,1:T(2,128)(2,1)S(1)} %get-tuple-element.621), channel_id=1, source_target_pairs={{0,14},{1,15},{2,0},{3,1},{4,2},{5,3},{6,4},{7,5},{8,6},{9,7},{10,... | collective-permute-start | bytes 30728 | tf_op jit(solution)/shard_map/while/body/eval_jaxpr/ppermute | solution.py:28
  110.7 11.9 %all-to-all-start = ((bf16[16,2,2560]{2,1,0:T(2,128)(2,1)}), bf16[16,2,2560]{2,1,0:T(2,128)(2,1)S(1)}, u32[]{:S(2)}, u32[]{:S(2)}) async-start(bf16[16,2,2560]{2,1,0:T(2,128)(2,1)} %reshape.335), calls=%async_computation | async-start | bytes 327680 | tf_op jit(solution)/shard_map/while/body/eval_jaxpr/all_to_all | solution.py:90
  (20 other events, 333.5 us)
Sparse Core Ops, SparseCore 0:
  125.8 24.1 all-reduce.1
